TPU v7x, 32 devices: a whole 2x2x4 slice. The times are simulated.
32 devices in a mesh: ens: 2 (over y), lon: 4 (over z), dom: 4 (over x, core).
Axes of the slice: x: 2, y: 2, z: 4, core: 2. Of those that a mesh axis runs over, the one named last changes fastest.
Arguments:
- particles: bfloat16 [16, 69, 96, 256], P(('ens', 'dom'), None, 'lon'), parts along dimension 0, may hold values from -6 to 6
- observed: bfloat16 [138, 96, 256], P('ens', 'lon'), parts along dimension 0, may hold values from -6 to 6
- precision: float32 [192, 256], P(('ens', 'lon')), parts along dimension 0, may hold values from 0.25 to 12, as said below
- stations: int32 [192, 256], P(('ens', 'lon')), parts along dimension 0, may hold values 0 or 1
- ancestors: int32 [16], P(('ens', 'dom')), parts along dimension 0, may hold values from 0 to 7
- tempering: float32 [2], P('ens'), parts along dimension 0, may hold values from 1 to 4
- w_in: bfloat16 [3, 3, 64, 69], replicated, may hold values from -0.25 to 0.25
- w_mid: bfloat16 [3, 3, 64, 64], replicated, may hold values from -0.25 to 0.25
- w_out: bfloat16 [3, 3, 69, 64], replicated, may hold values from -0.25 to 0.25
Outputs:
- new_particles: bfloat16 [16, 69, 96, 256], P(('ens', 'dom'), None, 'lon'), parts along dimension 0
- weights: float32 [16], P(('ens', 'dom')), parts along dimension 0
There are 2 independent parts, one for each index of `ens`. A program takes and returns all parts, laid end to end along the dimension named above; an argument that names none is the same for every part. Nothing has to cross between parts.
Inputs may be any that keep to these rules, and one draw needn't show every extreme that they name: `precision`: positive everywhere; no other structure is promised. Slot s continues particle ancestors[s]; a particle may be continued by several slots or by none.
All inputs are finite; a program needn't handle non-finite values. No bound on the sum of `stations` on one device may be relied on, other than what follows from the above.
Results may differ from a plain program's by a relative error of at most 0.0021.
Values may be sent and summed in bfloat16 or wider, within the bound.
A program may use at most 128 MiB of HBM per device.

v0:
```python
import jax
import jax.numpy as jnp
from jax import lax
from jax.sharding import PartitionSpec as P


def extended_2(block, sides, width):
    for axis, dim in sides:
        count = lax.axis_size(axis)
        forward = [(i, i + 1) for i in range(count - 1)]
        forward.append((count - 1, 0))
        backward = [(target, source) for source, target in forward]
        low = lax.ppermute(
            lax.slice_in_dim(block, block.shape[dim] - width, None, axis=dim), axis, forward
        )
        high = lax.ppermute(lax.slice_in_dim(block, 0, width, axis=dim), axis, backward)
        block = jnp.concatenate([low, block, high], axis=dim)
    return block


def conv_local(extended, weight):
    out_width = extended.shape[2] - 2
    lat_rows = extended.shape[3]
    padded = jnp.pad(extended, ((0, 0), (0, 0), (0, 0), (1, 1)))
    summed = jnp.zeros((extended.shape[0], weight.shape[2], out_width, lat_rows), jnp.float32)
    for row_tap in range(3):
        for col_tap in range(3):
            window = padded[:, :, row_tap : row_tap + out_width, col_tap : col_tap + lat_rows]
            summed = summed + jnp.einsum(
                "oc,pcxy->poxy",
                weight[row_tap, col_tap],
                window,
                preferred_element_type=jnp.float32,
            )
    return summed


def denoise_local(states, observed, obs_weight, w_in, w_mid, w_out):
    extended = extended_2(states, (("lon", 2),), 1)
    first_act = jax.nn.silu(conv_local(extended, w_in)).astype(jnp.bfloat16)
    first_ext = extended_2(first_act, (("lon", 2),), 1)
    second_act = jax.nn.silu(conv_local(first_ext, w_mid)).astype(jnp.bfloat16)
    second_ext = extended_2(second_act, (("lon", 2),), 1)
    noise_pred = conv_local(second_ext, w_out)
    current = states.astype(jnp.float32)
    updated = (
        current
        - 0.5 * noise_pred
        + 0.25 * obs_weight[None, None] * (observed.astype(jnp.float32)[None] - current)
    )
    return updated.astype(jnp.bfloat16)


def continue_slots(slabs, slot_ancestors):
    slab_piece = lax.all_gather(slabs, "dom", axis=0, tiled=True)
    piece_rows = slab_piece.shape[0]
    inside = (slot_ancestors >= 0) & (slot_ancestors < piece_rows)
    chosen = jnp.take(slab_piece, jnp.clip(slot_ancestors, 0, piece_rows - 1), axis=0)
    return jnp.where(inside[:, None, None, None], chosen, jnp.zeros_like(slabs))


def on_device(particles, observed, precision, stations, ancestors, tempering, w_in, w_mid, w_out):
    obs_weight = stations.astype(jnp.float32) * precision
    misfit_cell = particles.astype(jnp.float32) - observed.astype(jnp.float32)[None]
    local_sums = jnp.sum(obs_weight[None, None] * misfit_cell * misfit_cell, axis=(1, 2, 3))
    band_sums = lax.psum(local_sums, "lon")
    every_sum = lax.all_gather(band_sums, "dom", axis=0, tiled=True)
    center = jnp.mean(every_sum)
    deviation = every_sum - center
    spread = jnp.sqrt(jnp.mean(deviation * deviation) + 1.0)
    log_weights = -0.5 * tempering[0] * deviation / spread
    expo = jnp.exp(log_weights)
    weights_all = expo / jnp.sum(expo)
    slot_count = ancestors.shape[0]
    own_weights = lax.dynamic_slice_in_dim(
        weights_all, lax.axis_index("dom") * slot_count, slot_count
    )
    continued = continue_slots(particles, ancestors)
    new_particles = denoise_local(continued, observed, obs_weight, w_in, w_mid, w_out)
    return (new_particles, own_weights)


def solution(mesh):
    return jax.shard_map(
        on_device,
        mesh=mesh,
        in_specs=(
            P(("ens", "dom"), None, "lon", None),
            P("ens", "lon", None),
            P(("ens", "lon"), None),
            P(("ens", "lon"), None),
            P(("ens", "dom")),
            P("ens"),
            P(),
            P(),
            P(),
        ),
        out_specs=(P(("ens", "dom"), None, "lon", None), P(("ens", "dom"))),
        check_vma=False,
    )
```

profile of v0, /device:TPU:0, one launch (start us, length us, event | category | flops | bytes accessed | tf_op | source)
XLA Modules:
  0.0 159.0 jit_solution(17750243368687318687)
XLA Ops:
  10.2 13.4 %psum.7 = f32[2]{0:T(128)S(1)} all-reduce(f32[2]{0:T(128)S(1)} %fusion.5), channel_id=1, replica_groups=mesh['ens'=2,'lon'=4,'dom'=4] {'lon'}, use_global_device_ids=true, to_apply=%region_1.0 | all-reduce | flops 2 | bytes 16 | tf_op jit(solution)/shard_map/psum | solution.py:66
  25.1 6.1 %all-reduce.3 = f32[8]{0:T(128)S(1)} all-reduce(f32[8]{0:T(128)S(1)} %dynamic-update-slice), channel_id=1, replica_groups=mesh['ens'=2,'lon'=4,'dom'=4] {'dom'}, use_global_device_ids=true, to_apply=%add.3 | all-reduce | flops 8 | bytes 64
  36.4 25.2 %all-gather.2.cloned.1.call-done = bf16[8,69,24,256]{3,2,1,0:T(8,128)(2,1)} async-done(((bf16[2,69,24,256]{3,2,1,0:T(8,128)(2,1)}), bf16[8,69,24,256]{3,2,1,0:T(8,128)(2,1)}) %all-gather.2.cloned.1.call-update) | async-done | bytes 6782992 | tf_op jit(solution)/shard_map/all_gather | solution.py:55
  61.6 3.6 %gather_fusion = bf16[2,69,24,256]{3,2,1,0:T(8,128)(2,1)S(1)} fusion(bf16[8,69,24,256]{3,2,1,0:T(8,128)(2,1)} %all-gather.2.cloned.1.call-done, s32[1024]{0:T(1024)S(1)} %pad_clamp_fusion), kind=kCustom, calls=%fused_computation | custom fusion | bytes 3391496 | tf_op jit(solution)/shard_map/jit(_take)/gather | solution.py:58
  65.7 1.5 collective-permute-start
  67.2 2.3 %collective-permute-start.1 = (bf16[2,69,1,256]{3,1,2,0:T(8,128)(2,1)S(1)}, bf16[2,69,1,256]{3,1,2,0:T(8,128)(2,1)S(1)}, u32[]{:S(2)}, u32[]{:S(2)}) collective-permute-start(bf16[2,69,1,256]{3,1,2,0:T(8,128)(2,1)S(1)} %get-tuple-element.15), channel_id=1, source_target_pairs={{4,0},{8,4},{12,8},{0,12},{5,1},{9,5},{13,9},{1,13},{6,2},{10,6},{... | collective-permute-start | bytes 211976 | tf_op jit(solution)/shard_map/ppermute | solution.py:16
  69.6 2.6 %fusion.111 = f32[2,24,256,64]{2,3,1,0:T(8,128)} fusion(bf16[3,3,64,69]{3,2,1,0:T(8,128)(2,1)S(1)} %copy-done.3, bf16[2,69,24,256]{3,2,1,0:T(8,128)(2,1)S(1)} %gather_fusion, pred[2]{0:T(512)(128)(4,1)S(1)} %get-tuple-element.12, pred[2]{0:T(512)(128)(4,1)S(1)} %get-tuple-element.20), kind=kOutput, calls=%fused_computation.123 | convolution fusion | flops 110223360 | bytes 4858880 | tf_op jit(solution)/shard_map/oc,pcxy->poxy/dot_general | solution.py:29
  73.0 2.0 %fusion.18 = bf16[2,69,26,258]{3,1,2,0:T(8,128)(2,1)S(1)} fusion(bf16[2,69,1,256]{3,1,2,0:T(8,128)(2,1)S(1)} %collective-permute-done.1, bf16[2,69,24,256]{3,1,2,0:T(8,128)(2,1)S(1)} %fusion.44, bf16[2,69,1,256]{3,1,2,0:T(8,128)(2,1)S(1)} %collective-permute-done), kind=kLoop, calls=%fused_computation.30 | loop fusion | flops 11108448 | bytes 3688464 | tf_op jit(solution)/shard_map/concatenate | solution.py:17
  77.8 2.2 %fusion.42 = f32[2,24,256,64]{2,3,1,0:T(8,128)} fusion(bf16[2,69,26,258]{3,1,2,0:T(8,128)(2,1)S(1)} %fusion.18, bf16[3,3,64,69]{3,2,1,0:T(8,128)(2,1)S(1)} %copy-done.3), kind=kOutput, calls=%fused_computation.56 | convolution fusion | flops 108527616 | bytes 4931584 | tf_op jit(solution)/shard_map/oc,pcxy->poxy/dot_general | solution.py:29
  80.0 2.2 %fusion.24 = f32[2,24,256,64]{2,3,1,0:T(8,128)} fusion(bf16[2,69,24,256]{3,1,2,0:T(8,128)(2,1)S(1)} %fusion.44, bf16[2,69,1,256]{3,1,2,0:T(8,128)(2,1)S(1)} %collective-permute-done, bf16[3,3,64,69]{3,2,1,0:T(8,128)(2,1)S(1)} %copy-done.3), kind=kOutput, calls=%fused_computation.38 | convolution fusion | flops 112060416 | bytes 5005312 | tf_op jit(solution)/shard_map/oc,pcxy->poxy/dot_general | solution.py:29
  82.2 2.2 %fusion.28 = f32[2,24,256,64]{2,3,1,0:T(8,128)} fusion(bf16[2,69,1,256]{3,1,2,0:T(8,128)(2,1)S(1)} %collective-permute-done.1, bf16[2,69,24,256]{3,1,2,0:T(8,128)(2,1)S(1)} %fusion.44, bf16[3,3,64,69]{3,2,1,0:T(8,128)(2,1)S(1)} %copy-done.3), kind=kOutput, calls=%fused_computation.42 | convolution fusion | flops 112060416 | bytes 5005312 | tf_op jit(solution)/shard_map/oc,pcxy->poxy/dot_general | solution.py:29
  84.4 6.0 %fusion.15 = bf16[2,64,24,256]{3,1,2,0:T(8,128)(2,1)S(1)} fusion(f32[2,24,256,64]{2,3,1,0:T(8,128)} %fusion.28, f32[2,24,256,64]{2,3,1,0:T(8,128)S(1)} %fusion.34, f32[2,24,256,64]{2,3,1,0:T(8,128)S(1)} %fusion.36, f32[2,24,256,64]{2,3,1,0:T(8,128)} %fusion.111, f32[2,24,256,64]{2,3,1,0:T(8,128)S(1)} %fusion.38, f32[2,24,256,64]{2,3,1,0:T(8,128)S(1)} %fusion.40, ...), kind=kOutput, calls=%fused_computation.27 | convolution fusion | flops 118751232 | bytes 28524544 | tf_op jit(solution)/shard_map/oc,pcxy->poxy/dot_general | solution.py:29
  91.6 2.7 %collective-permute-start.3 = (bf16[2,64,1,256]{3,1,2,0:T(8,128)(2,1)S(1)}, bf16[2,64,1,256]{3,1,2,0:T(8,128)(2,1)S(1)}, u32[]{:S(2)}, u32[]{:S(2)}) collective-permute-start(bf16[2,64,1,256]{3,1,2,0:T(8,128)(2,1)S(1)} %get-tuple-element.19), channel_id=1, source_target_pairs={{4,0},{8,4},{12,8},{0,12},{5,1},{9,5},{13,9},{1,13},{6,2},{10,6},{... | collective-permute-start | bytes 196616 | tf_op jit(solution)/shard_map/ppermute | solution.py:16
  94.9 1.8 %collective-permute-done.2 = bf16[2,64,1,256]{3,1,2,0:T(8,128)(2,1)S(1)} collective-permute-done((bf16[2,64,1,256]{3,1,2,0:T(8,128)(2,1)S(1)}, bf16[2,64,1,256]{3,1,2,0:T(8,128)(2,1)S(1)}, u32[]{:S(2)}, u32[]{:S(2)}) %collective-permute-start.2) | collective-permute-done | bytes 65568 | tf_op jit(solution)/shard_map/ppermute | solution.py:13
  96.8 1.8 %fusion.23 = bf16[2,64,26,258]{3,1,2,0:T(8,128)(2,1)S(1)} fusion(bf16[2,64,1,256]{3,1,2,0:T(8,128)(2,1)S(1)} %collective-permute-done.3, bf16[2,64,24,256]{3,1,2,0:T(8,128)(2,1)S(1)} %fusion.15, bf16[2,64,1,256]{3,1,2,0:T(8,128)(2,1)S(1)} %collective-permute-done.2), kind=kLoop, calls=%fused_computation.37 | loop fusion | flops 10303488 | bytes 3421184 | tf_op jit(solution)/shard_map/concatenate | solution.py:17
  100.4 2.3 %fusion.81 = f32[2,24,256,64]{2,3,1,0:T(8,128)} fusion(bf16[2,64,26,258]{3,1,2,0:T(8,128)(2,1)S(1)} %fusion.23, bf16[3,3,64,64]{3,2,1,0:T(8,128)(2,1)S(1)} %copy-done.1), kind=kOutput, calls=%fused_computation.91 | convolution fusion | flops 100663296 | bytes 4734976 | tf_op jit(solution)/shard_map/oc,pcxy->poxy/dot_general | solution.py:29
  102.7 2.2 %fusion.85 = f32[2,24,256,64]{2,3,1,0:T(8,128)} fusion(bf16[2,64,26,258]{3,1,2,0:T(8,128)(2,1)S(1)} %fusion.23, bf16[3,3,64,64]{3,2,1,0:T(8,128)(2,1)S(1)} %copy-done.1), kind=kOutput, calls=%fused_computation.96 | convolution fusion | flops 100663296 | bytes 4734976 | tf_op jit(solution)/shard_map/oc,pcxy->poxy/dot_general | solution.py:29
  104.9 2.2 %fusion.83 = f32[2,24,256,64]{2,3,1,0:T(8,128)} fusion(bf16[2,64,24,256]{3,1,2,0:T(8,128)(2,1)S(1)} %fusion.15, bf16[2,64,1,256]{3,1,2,0:T(8,128)(2,1)S(1)} %collective-permute-done.2, bf16[3,3,64,64]{3,2,1,0:T(8,128)(2,1)S(1)} %copy-done.1), kind=kOutput, calls=%fused_computation.94 | convolution fusion | flops 103809024 | bytes 4800512 | tf_op jit(solution)/shard_map/oc,pcxy->poxy/dot_general | solution.py:29
  107.1 2.2 %fusion.73 = f32[2,24,256,64]{2,3,1,0:T(8,128)} fusion(bf16[2,64,1,256]{3,1,2,0:T(8,128)(2,1)S(1)} %collective-permute-done.3, bf16[2,64,24,256]{3,1,2,0:T(8,128)(2,1)S(1)} %fusion.15, bf16[3,3,64,64]{3,2,1,0:T(8,128)(2,1)S(1)} %copy-done.1), kind=kOutput, calls=%fused_computation.83 | convolution fusion | flops 103809024 | bytes 4800512 | tf_op jit(solution)/shard_map/oc,pcxy->poxy/dot_general | solution.py:29
  109.3 5.9 %fusion.16 = bf16[2,64,24,256]{3,1,2,0:T(8,128)(2,1)S(1)} fusion(f32[2,24,256,64]{2,3,1,0:T(8,128)} %fusion.73, f32[2,24,256,64]{2,3,1,0:T(8,128)S(1)} %fusion.75, f32[2,24,256,64]{2,3,1,0:T(8,128)S(1)} %fusion.77, f32[2,24,256,64]{2,3,1,0:T(8,128)S(1)} %fusion.101, f32[2,24,256,64]{2,3,1,0:T(8,128)S(1)} %fusion.79, f32[2,24,256,64]{2,3,1,0:T(8,128)} %fusion.81, ...), kind=kOutput, calls=%fused_computation.28 | convolution fusion | flops 110886912 | bytes 28327936 | tf_op jit(solution)/shard_map/oc,pcxy->poxy/dot_general | solution.py:29
  115.9 3.3 %collective-permute-start.5 = (bf16[2,64,1,256]{3,1,2,0:T(8,128)(2,1)S(1)}, bf16[2,64,1,256]{3,1,2,0:T(8,128)(2,1)S(1)}, u32[]{:S(2)}, u32[]{:S(2)}) collective-permute-start(bf16[2,64,1,256]{3,1,2,0:T(8,128)(2,1)S(1)} %get-tuple-element.17), channel_id=1, source_target_pairs={{4,0},{8,4},{12,8},{0,12},{5,1},{9,5},{13,9},{1,13},{6,2},{10,6},{... | collective-permute-start | bytes 196616 | tf_op jit(solution)/shard_map/ppermute | solution.py:16
  119.9 1.6 collective-permute-done.4
  121.4 1.8 %select_maximum_fusion = bf16[2,64,26,258]{3,1,2,0:T(8,128)(2,1)S(1)} fusion(bf16[2,64,1,256]{3,1,2,0:T(8,128)(2,1)S(1)} %collective-permute-done.5, bf16[2,64,24,256]{3,1,2,0:T(8,128)(2,1)S(1)} %fusion.16, bf16[2,64,1,256]{3,1,2,0:T(8,128)(2,1)S(1)} %collective-permute-done.4), kind=kLoop, calls=%fused_computation.31 | loop fusion | flops 10303488 | bytes 3421184 | tf_op jit(solution)/shard_map/concatenate | solution.py:17
  123.2 2.5 %fusion.59 = f32[2,24,256,69]{2,3,1,0:T(8,128)} fusion(bf16[2,64,26,258]{3,1,2,0:T(8,128)(2,1)S(1)} %select_maximum_fusion, bf16[3,3,69,64]{2,3,1,0:T(8,128)(2,1)S(1)} %copy-done.2), kind=kOutput, calls=%fused_computation.70 | convolution fusion | flops 108527616 | bytes 4980736 | tf_op jit(solution)/shard_map/oc,pcxy->poxy/dot_general | solution.py:29
  125.7 2.6 %fusion.61 = f32[2,24,256,69]{2,3,1,0:T(8,128)} fusion(bf16[2,64,26,258]{3,1,2,0:T(8,128)(2,1)S(1)} %select_maximum_fusion, bf16[3,3,69,64]{2,3,1,0:T(8,128)(2,1)S(1)} %copy-done.2), kind=kOutput, calls=%fused_computation.72 | convolution fusion | flops 108527616 | bytes 4980736 | tf_op jit(solution)/shard_map/oc,pcxy->poxy/dot_general | solution.py:29
  128.2 2.5 %fusion.63 = f32[2,24,256,69]{2,3,1,0:T(8,128)} fusion(bf16[2,64,26,258]{3,1,2,0:T(8,128)(2,1)S(1)} %select_maximum_fusion, bf16[3,3,69,64]{2,3,1,0:T(8,128)(2,1)S(1)} %copy-done.2), kind=kOutput, calls=%fused_computation.74 | convolution fusion | flops 108527616 | bytes 4980736 | tf_op jit(solution)/shard_map/oc,pcxy->poxy/dot_general | solution.py:29
  130.8 2.5 %fusion.65 = f32[2,24,256,69]{2,3,1,0:T(8,128)} fusion(bf16[2,64,26,258]{3,1,2,0:T(8,128)(2,1)S(1)} %select_maximum_fusion, bf16[3,3,69,64]{2,3,1,0:T(8,128)(2,1)S(1)} %copy-done.2), kind=kOutput, calls=%fused_computation.76 | convolution fusion | flops 108527616 | bytes 4980736 | tf_op jit(solution)/shard_map/oc,pcxy->poxy/dot_general | solution.py:29
  133.3 2.4 %fusion.67 = f32[2,24,256,69]{2,3,1,0:T(8,128)} fusion(bf16[2,64,26,258]{3,1,2,0:T(8,128)(2,1)S(1)} %select_maximum_fusion, bf16[3,3,69,64]{2,3,1,0:T(8,128)(2,1)S(1)} %copy-done.2), kind=kOutput, calls=%fused_computation.78 | convolution fusion | flops 108527616 | bytes 4980736 | tf_op jit(solution)/shard_map/oc,pcxy->poxy/dot_general | solution.py:29
  135.7 2.4 %fusion.47 = f32[2,24,256,69]{2,3,1,0:T(8,128)} fusion(bf16[2,64,24,256]{3,1,2,0:T(8,128)(2,1)S(1)} %fusion.16, bf16[2,64,1,256]{3,1,2,0:T(8,128)(2,1)S(1)} %collective-permute-done.4, bf16[3,3,69,64]{2,3,1,0:T(8,128)(2,1)S(1)} %copy-done.2), kind=kOutput, calls=%fused_computation.60 | convolution fusion | flops 111804416 | bytes 5046272 | tf_op jit(solution)/shard_map/oc,pcxy->poxy/dot_general | solution.py:29
  138.1 2.4 %fusion.51 = f32[2,24,256,69]{2,3,1,0:T(8,128)} fusion(bf16[2,64,1,256]{3,1,2,0:T(8,128)(2,1)S(1)} %collective-permute-done.5, bf16[2,64,24,256]{3,1,2,0:T(8,128)(2,1)S(1)} %fusion.16, bf16[3,3,69,64]{2,3,1,0:T(8,128)(2,1)S(1)} %copy-done.2), kind=kOutput, calls=%fused_computation.64 | convolution fusion | flops 111804416 | bytes 5046272 | tf_op jit(solution)/shard_map/oc,pcxy->poxy/dot_general | solution.py:29
  140.5 10.1 %fusion.3 = bf16[2,69,24,256]{3,1,2,0:T(8,128)(2,1)S(1)} fusion(f32[2,24,256,69]{2,3,1,0:T(8,128)} %fusion.51, f32[2,24,256,69]{2,3,1,0:T(8,128)} %fusion.59, f32[2,24,256,69]{2,3,1,0:T(8,128)} %fusion.61, f32[2,24,256,69]{2,3,1,0:T(8,128)S(1)} %fusion.91, f32[2,24,256,69]{2,3,1,0:T(8,128)} %fusion.63, f32[2,24,256,69]{2,3,1,0:T(8,128)} %fusion.65, ...), kind=kOutput, calls=%fused_computation.11 | convolution fusion | flops 122941440 | bytes 34055168 | tf_op jit(solution)/shard_map/oc,pcxy->poxy/dot_general | solution.py:29
  150.6 1.5 copy.21
  (50 shorter events, 15.7 us)
Async XLA Ops:
  7.2 2.2 %copy-start = (bf16[2,69,24,256]{3,2,1,0:T(8,128)(2,1)S(1)}, bf16[2,69,24,256]{3,2,1,0:T(8,128)(2,1)}, u32[]{:S(2)}) copy-start(bf16[2,69,24,256]{3,2,1,0:T(8,128)(2,1)} %param.9) | copy-start | bytes 5087236
  7.2 2.1 %copy-start.5 = (s32[24,256]{1,0:T(8,128)S(1)}, s32[24,256]{1,0:T(8,128)}, u32[]{:S(2)}) copy-start(s32[24,256]{1,0:T(8,128)} %param.12) | copy-start | bytes 73732
  7.2 2.1 %copy-start.4 = (f32[24,256]{1,0:T(8,128)S(1)}, f32[24,256]{1,0:T(8,128)}, u32[]{:S(2)}) copy-start(f32[24,256]{1,0:T(8,128)} %param.11) | copy-start | bytes 73732
  7.2 54.4 %all-gather.2.cloned.1.call-start = ((), (), s32[]{:S(2)}) async-start(), calls=%async_computation | async-start | bytes 8478720 | tf_op jit(solution)/shard_map/all_gather | solution.py:55
  7.9 15.7 %copy-start.7 = (u32[32]{0:T(128)S(1)}, u32[32]{0:T(128)}, u32[]{:S(2)}) copy-start(u32[32]{0:T(128)} %constant.60) | copy-start | bytes 388
  7.9 28.4 %copy-start.6 = (s32[2]{0:T(128)S(1)}, s32[2]{0:T(128)}, u32[]{:S(2)}) copy-start(s32[2]{0:T(128)} %param.13) | copy-start | bytes 28
  65.2 4.4 %copy-start.3 = (bf16[3,3,64,69]{3,2,1,0:T(8,128)(2,1)S(1)}, bf16[3,3,64,69]{3,2,1,0:T(8,128)(2,1)}, u32[]{:S(2)}) copy-start(bf16[3,3,64,69]{3,2,1,0:T(8,128)(2,1)} %param.15) | copy-start | bytes 238468
  65.7 6.7 %collective-permute-start = (bf16[2,69,1,256]{3,1,2,0:T(8,128)(2,1)S(1)}, bf16[2,69,1,256]{3,1,2,0:T(8,128)(2,1)S(1)}, u32[]{:S(2)}, u32[]{:S(2)}) collective-permute-start(bf16[2,69,1,256]{3,1,2,0:T(8,128)(2,1)S(1)} %get-tuple-element.14), channel_id=1, source_target_pairs={{0,4},{4,8},{8,12},{12,0},{1,5},{5,9},{9,13},{13,1},{2,6},{6,10},{... | collective-permute-start | bytes 211976 | tf_op jit(solution)/shard_map/ppermute | solution.py:13
  67.2 5.7 %collective-permute-start.1 = (bf16[2,69,1,256]{3,1,2,0:T(8,128)(2,1)S(1)}, bf16[2,69,1,256]{3,1,2,0:T(8,128)(2,1)S(1)}, u32[]{:S(2)}, u32[]{:S(2)}) collective-permute-start(bf16[2,69,1,256]{3,1,2,0:T(8,128)(2,1)S(1)} %get-tuple-element.15), channel_id=1, source_target_pairs={{4,0},{8,4},{12,8},{0,12},{5,1},{9,5},{13,9},{1,13},{6,2},{10,6},{... | collective-permute-start | bytes 211976 | tf_op jit(solution)/shard_map/ppermute | solution.py:16
  84.4 9.9 %copy-start.1 = (bf16[3,3,64,64]{3,2,1,0:T(8,128)(2,1)S(1)}, bf16[3,3,64,64]{3,2,1,0:T(8,128)(2,1)}, u32[]{:S(2)}) copy-start(bf16[3,3,64,64]{3,2,1,0:T(8,128)(2,1)} %param.16) | copy-start | bytes 221188
  90.4 6.3 %collective-permute-start.2 = (bf16[2,64,1,256]{3,1,2,0:T(8,128)(2,1)S(1)}, bf16[2,64,1,256]{3,1,2,0:T(8,128)(2,1)S(1)}, u32[]{:S(2)}, u32[]{:S(2)}) collective-permute-start(bf16[2,64,1,256]{3,1,2,0:T(8,128)(2,1)S(1)} %get-tuple-element.18), channel_id=1, source_target_pairs={{0,4},{4,8},{8,12},{12,0},{1,5},{5,9},{9,13},{13,1},{2,6},{6,10},{... | collective-permute-start | bytes 196616 | tf_op jit(solution)/shard_map/ppermute | solution.py:13
  91.6 5.2 %collective-permute-start.3 = (bf16[2,64,1,256]{3,1,2,0:T(8,128)(2,1)S(1)}, bf16[2,64,1,256]{3,1,2,0:T(8,128)(2,1)S(1)}, u32[]{:S(2)}, u32[]{:S(2)}) collective-permute-start(bf16[2,64,1,256]{3,1,2,0:T(8,128)(2,1)S(1)} %get-tuple-element.19), channel_id=1, source_target_pairs={{4,0},{8,4},{12,8},{0,12},{5,1},{9,5},{13,9},{1,13},{6,2},{10,6},{... | collective-permute-start | bytes 196616 | tf_op jit(solution)/shard_map/ppermute | solution.py:16
  109.3 9.9 %copy-start.2 = (bf16[3,3,69,64]{2,3,1,0:T(8,128)(2,1)S(1)}, bf16[3,3,69,64]{2,3,1,0:T(8,128)(2,1)}, u32[]{:S(2)}) copy-start(bf16[3,3,69,64]{2,3,1,0:T(8,128)(2,1)} %param.17) | copy-start | bytes 238468
  115.3 6.2 %collective-permute-start.4 = (bf16[2,64,1,256]{3,1,2,0:T(8,128)(2,1)S(1)}, bf16[2,64,1,256]{3,1,2,0:T(8,128)(2,1)S(1)}, u32[]{:S(2)}, u32[]{:S(2)}) collective-permute-start(bf16[2,64,1,256]{3,1,2,0:T(8,128)(2,1)S(1)} %get-tuple-element.16), channel_id=1, source_target_pairs={{0,4},{4,8},{8,12},{12,0},{1,5},{5,9},{9,13},{13,1},{2,6},{6,10},{... | collective-permute-start | bytes 196616 | tf_op jit(solution)/shard_map/ppermute | solution.py:13
  115.9 5.6 %collective-permute-start.5 = (bf16[2,64,1,256]{3,1,2,0:T(8,128)(2,1)S(1)}, bf16[2,64,1,256]{3,1,2,0:T(8,128)(2,1)S(1)}, u32[]{:S(2)}, u32[]{:S(2)}) collective-permute-start(bf16[2,64,1,256]{3,1,2,0:T(8,128)(2,1)S(1)} %get-tuple-element.17), channel_id=1, source_target_pairs={{4,0},{8,4},{12,8},{0,12},{5,1},{9,5},{13,9},{1,13},{6,2},{10,6},{... | collective-permute-start | bytes 196616 | tf_op jit(solution)/shard_map/ppermute | solution.py:16
Sparse Core Ops, SparseCore 0:
  9.6 51.9 all-gather.1
where the time goes:
time: 159 us
  matrix products  63.2 us (40%)
  waiting for transfers between devices  30.2 us (19%)
  blocking collectives  19.6 us (12%)
  between operations  16.9 us (11%)
  starting transfers between devices  11.7 us (7%)
  other arithmetic  9.41 us (6%)
  local copies, waits for them, and re-layouts  7.92 us (5%)
    dot_general x27, matrix products, conv_local(): jnp.einsum('oc,pcxy->poxy', weight[row_tap, col_tap], window, preferred_e...  63.2 us
    all_gather x1, waiting for transfers between devices, continue_slots(): slab_piece = lax.all_gather(slabs, 'dom', axis=0, tiled=True)  25.2 us
    psum x1, blocking collectives, on_device(): band_sums = lax.psum(local_sums, 'lon')  13.4 us
    ppermute x3, starting transfers between devices, extended_2(): lax.ppermute(lax.slice_in_dim(block, 0, width, axis=dim), axis, backward)  8.36 us
    unnamed x1, blocking collectives  6.14 us
    concatenate x3, other arithmetic, extended_2(): block = jnp.concatenate([low, block, high], axis=dim)  5.59 us
    ppermute x3, waiting for transfers between devices, extended_2(): lax.ppermute(lax.slice_in_dim(block, block.shape[dim] - width, None, axis...  3.61 us
    gather x1, local copies, waits for them, and re-layouts, continue_slots(): jnp.take(slab_piece, jnp.clip(slot_ancestors, 0, piece_rows - 1), axis=0)  3.58 us
  transfers between devices with their start and end apart: 7, of which 6 were waited for; matrix products, arithmetic and copies ran while one was open for 6% of the time, Pallas kernels for 0%

commit v1 on v0

--- a/solution.py
+++ b/solution.py
@@ -63,7 +63,7 @@
     obs_weight = stations.astype(jnp.float32) * precision
     misfit_cell = particles.astype(jnp.float32) - observed.astype(jnp.float32)[None]
     local_sums = jnp.sum(obs_weight[None, None] * misfit_cell * misfit_cell, axis=(1, 2, 3))
-    band_sums = lax.psum(local_sums, "lon")
+    band_sums = jnp.sum(lax.all_gather(local_sums, "lon"), axis=0)
     every_sum = lax.all_gather(band_sums, "dom", axis=0, tiled=True)
     center = jnp.mean(every_sum)
     deviation = every_sum - center

time: 159 us -> 159 us (level)
    psum x1 -> x0, blocking collectives: 13.4 us -> none  [on_device(): band_sums = lax.psum(local_sums, 'lon')]
    unnamed x1 -> x2, blocking collectives: 6.14 us -> 19.6 us
  transfers between devices with their start and end apart: 7 -> 7, of which waited for: 6 -> 6; matrix products, arithmetic and copies ran while one was open for 6% -> 7% of each run, Pallas kernels for 0% -> 0%
where the time goes in v1:
time: 159 us
  matrix products  63.2 us (40%)
  waiting for transfers between devices  28.7 us (18%)
  blocking collectives  19.6 us (12%)
  between operations  17.6 us (11%)
  starting transfers between devices  11.7 us (7%)
  other arithmetic  9.43 us (6%)
  local copies, waits for them, and re-layouts  8.78 us (6%)
    dot_general x27, matrix products, conv_local(): jnp.einsum('oc,pcxy->poxy', weight[row_tap, col_tap], window, preferred_e...  63.2 us
    all_gather x1, waiting for transfers between devices, continue_slots(): slab_piece = lax.all_gather(slabs, 'dom', axis=0, tiled=True)  23.7 us
    unnamed x2, blocking collectives  19.6 us
    ppermute x3, starting transfers between devices, extended_2(): lax.ppermute(lax.slice_in_dim(block, 0, width, axis=dim), axis, backward)  8.37 us
    concatenate x3, other arithmetic, extended_2(): block = jnp.concatenate([low, block, high], axis=dim)  5.59 us
    ppermute x3, waiting for transfers between devices, extended_2(): lax.ppermute(lax.slice_in_dim(block, block.shape[dim] - width, None, axis...  3.64 us
    gather x1, local copies, waits for them, and re-layouts, continue_slots(): jnp.take(slab_piece, jnp.clip(slot_ancestors, 0, piece_rows - 1), axis=0)  3.58 us
    ppermute x3, starting transfers between devices, extended_2(): lax.ppermute(lax.slice_in_dim(block, block.shape[dim] - width, None, axis...  3.3 us
  transfers between devices with their start and end apart: 7, of which 6 were waited for; matrix products, arithmetic and copies ran while one was open for 7% of the time, Pallas kernels for 0%

profile of v1, /device:TPU:0, one launch (start us, length us, event | category | flops | bytes accessed | tf_op | source)
XLA Modules:
  0.0 159.0 jit_solution(16034325286232587705)
XLA Ops:
  11.7 13.4 %all-reduce.3 = f32[8]{0:T(128)S(1)} all-reduce(f32[8]{0:T(128)S(1)} %dynamic-update-slice), channel_id=2, replica_groups=mesh['ens'=2,'lon'=4,'dom'=4] {'lon'}, use_global_device_ids=true, to_apply=%add.3 | all-reduce | flops 8 | bytes 64
  26.7 6.1 %all-reduce.4 = f32[8]{0:T(128)S(1)} all-reduce(f32[8]{0:T(128)S(1)} %dynamic-update-slice.1), channel_id=1, replica_groups=mesh['ens'=2,'lon'=4,'dom'=4] {'dom'}, use_global_device_ids=true, to_apply=%add.4 | all-reduce | flops 8 | bytes 64
  37.9 23.7 %all-gather.3.cloned.1.call-done = bf16[8,69,24,256]{3,2,1,0:T(8,128)(2,1)} async-done(((bf16[2,69,24,256]{3,2,1,0:T(8,128)(2,1)}), bf16[8,69,24,256]{3,2,1,0:T(8,128)(2,1)}) %all-gather.3.cloned.1.call-update) | async-done | bytes 6782992 | tf_op jit(solution)/shard_map/all_gather | solution.py:55
  61.6 3.6 %gather_fusion = bf16[2,69,24,256]{3,2,1,0:T(8,128)(2,1)S(1)} fusion(bf16[8,69,24,256]{3,2,1,0:T(8,128)(2,1)} %all-gather.3.cloned.1.call-done, s32[1024]{0:T(1024)S(1)} %pad_clamp_fusion), kind=kCustom, calls=%fused_computation | custom fusion | bytes 3391496 | tf_op jit(solution)/shard_map/jit(_take)/gather | solution.py:58
  65.7 1.5 collective-permute-start
  67.2 2.3 %collective-permute-start.1 = (bf16[2,69,1,256]{3,1,2,0:T(8,128)(2,1)S(1)}, bf16[2,69,1,256]{3,1,2,0:T(8,128)(2,1)S(1)}, u32[]{:S(2)}, u32[]{:S(2)}) collective-permute-start(bf16[2,69,1,256]{3,1,2,0:T(8,128)(2,1)S(1)} %get-tuple-element.15), channel_id=1, source_target_pairs={{4,0},{8,4},{12,8},{0,12},{5,1},{9,5},{13,9},{1,13},{6,2},{10,6},{... | collective-permute-start | bytes 211976 | tf_op jit(solution)/shard_map/ppermute | solution.py:16
  69.6 2.6 %fusion.111 = f32[2,24,256,64]{2,3,1,0:T(8,128)} fusion(bf16[3,3,64,69]{3,2,1,0:T(8,128)(2,1)S(1)} %copy-done.3, bf16[2,69,24,256]{3,2,1,0:T(8,128)(2,1)S(1)} %gather_fusion, pred[2]{0:T(512)(128)(4,1)S(1)} %get-tuple-element.12, pred[2]{0:T(512)(128)(4,1)S(1)} %get-tuple-element.20), kind=kOutput, calls=%fused_computation.123 | convolution fusion | flops 110223360 | bytes 4858880 | tf_op jit(solution)/shard_map/oc,pcxy->poxy/dot_general | solution.py:29
  73.0 2.0 %fusion.18 = bf16[2,69,26,258]{3,1,2,0:T(8,128)(2,1)S(1)} fusion(bf16[2,69,1,256]{3,1,2,0:T(8,128)(2,1)S(1)} %collective-permute-done.1, bf16[2,69,24,256]{3,1,2,0:T(8,128)(2,1)S(1)} %fusion.44, bf16[2,69,1,256]{3,1,2,0:T(8,128)(2,1)S(1)} %collective-permute-done), kind=kLoop, calls=%fused_computation.30 | loop fusion | flops 11108448 | bytes 3688464 | tf_op jit(solution)/shard_map/concatenate | solution.py:17
  77.8 2.3 %fusion.42 = f32[2,24,256,64]{2,3,1,0:T(8,128)} fusion(bf16[2,69,26,258]{3,1,2,0:T(8,128)(2,1)S(1)} %fusion.18, bf16[3,3,64,69]{3,2,1,0:T(8,128)(2,1)S(1)} %copy-done.3), kind=kOutput, calls=%fused_computation.56 | convolution fusion | flops 108527616 | bytes 4931584 | tf_op jit(solution)/shard_map/oc,pcxy->poxy/dot_general | solution.py:29
  80.0 2.2 %fusion.24 = f32[2,24,256,64]{2,3,1,0:T(8,128)} fusion(bf16[2,69,24,256]{3,1,2,0:T(8,128)(2,1)S(1)} %fusion.44, bf16[2,69,1,256]{3,1,2,0:T(8,128)(2,1)S(1)} %collective-permute-done, bf16[3,3,64,69]{3,2,1,0:T(8,128)(2,1)S(1)} %copy-done.3), kind=kOutput, calls=%fused_computation.38 | convolution fusion | flops 112060416 | bytes 5005312 | tf_op jit(solution)/shard_map/oc,pcxy->poxy/dot_general | solution.py:29
  82.2 2.2 %fusion.28 = f32[2,24,256,64]{2,3,1,0:T(8,128)} fusion(bf16[2,69,1,256]{3,1,2,0:T(8,128)(2,1)S(1)} %collective-permute-done.1, bf16[2,69,24,256]{3,1,2,0:T(8,128)(2,1)S(1)} %fusion.44, bf16[3,3,64,69]{3,2,1,0:T(8,128)(2,1)S(1)} %copy-done.3), kind=kOutput, calls=%fused_computation.42 | convolution fusion | flops 112060416 | bytes 5005312 | tf_op jit(solution)/shard_map/oc,pcxy->poxy/dot_general | solution.py:29
  84.4 6.0 %fusion.15 = bf16[2,64,24,256]{3,1,2,0:T(8,128)(2,1)S(1)} fusion(f32[2,24,256,64]{2,3,1,0:T(8,128)} %fusion.28, f32[2,24,256,64]{2,3,1,0:T(8,128)S(1)} %fusion.34, f32[2,24,256,64]{2,3,1,0:T(8,128)S(1)} %fusion.36, f32[2,24,256,64]{2,3,1,0:T(8,128)} %fusion.111, f32[2,24,256,64]{2,3,1,0:T(8,128)S(1)} %fusion.38, f32[2,24,256,64]{2,3,1,0:T(8,128)S(1)} %fusion.40, ...), kind=kOutput, calls=%fused_computation.27 | convolution fusion | flops 118751232 | bytes 28524544 | tf_op jit(solution)/shard_map/oc,pcxy->poxy/dot_general | solution.py:29
  91.6 2.7 %collective-permute-start.3 = (bf16[2,64,1,256]{3,1,2,0:T(8,128)(2,1)S(1)}, bf16[2,64,1,256]{3,1,2,0:T(8,128)(2,1)S(1)}, u32[]{:S(2)}, u32[]{:S(2)}) collective-permute-start(bf16[2,64,1,256]{3,1,2,0:T(8,128)(2,1)S(1)} %get-tuple-element.19), channel_id=1, source_target_pairs={{4,0},{8,4},{12,8},{0,12},{5,1},{9,5},{13,9},{1,13},{6,2},{10,6},{... | collective-permute-start | bytes 196616 | tf_op jit(solution)/shard_map/ppermute | solution.py:16
  94.9 1.8 %collective-permute-done.2 = bf16[2,64,1,256]{3,1,2,0:T(8,128)(2,1)S(1)} collective-permute-done((bf16[2,64,1,256]{3,1,2,0:T(8,128)(2,1)S(1)}, bf16[2,64,1,256]{3,1,2,0:T(8,128)(2,1)S(1)}, u32[]{:S(2)}, u32[]{:S(2)}) %collective-permute-start.2) | collective-permute-done | bytes 65568 | tf_op jit(solution)/shard_map/ppermute | solution.py:13
  96.8 1.8 %fusion.23 = bf16[2,64,26,258]{3,1,2,0:T(8,128)(2,1)S(1)} fusion(bf16[2,64,1,256]{3,1,2,0:T(8,128)(2,1)S(1)} %collective-permute-done.3, bf16[2,64,24,256]{3,1,2,0:T(8,128)(2,1)S(1)} %fusion.15, bf16[2,64,1,256]{3,1,2,0:T(8,128)(2,1)S(1)} %collective-permute-done.2), kind=kLoop, calls=%fused_computation.37 | loop fusion | flops 10303488 | bytes 3421184 | tf_op jit(solution)/shard_map/concatenate | solution.py:17
  100.4 2.3 %fusion.81 = f32[2,24,256,64]{2,3,1,0:T(8,128)} fusion(bf16[2,64,26,258]{3,1,2,0:T(8,128)(2,1)S(1)} %fusion.23, bf16[3,3,64,64]{3,2,1,0:T(8,128)(2,1)S(1)} %copy-done.1), kind=kOutput, calls=%fused_computation.91 | convolution fusion | flops 100663296 | bytes 4734976 | tf_op jit(solution)/shard_map/oc,pcxy->poxy/dot_general | solution.py:29
  102.7 2.3 %fusion.85 = f32[2,24,256,64]{2,3,1,0:T(8,128)} fusion(bf16[2,64,26,258]{3,1,2,0:T(8,128)(2,1)S(1)} %fusion.23, bf16[3,3,64,64]{3,2,1,0:T(8,128)(2,1)S(1)} %copy-done.1), kind=kOutput, calls=%fused_computation.96 | convolution fusion | flops 100663296 | bytes 4734976 | tf_op jit(solution)/shard_map/oc,pcxy->poxy/dot_general | solution.py:29
  105.0 2.2 %fusion.83 = f32[2,24,256,64]{2,3,1,0:T(8,128)} fusion(bf16[2,64,24,256]{3,1,2,0:T(8,128)(2,1)S(1)} %fusion.15, bf16[2,64,1,256]{3,1,2,0:T(8,128)(2,1)S(1)} %collective-permute-done.2, bf16[3,3,64,64]{3,2,1,0:T(8,128)(2,1)S(1)} %copy-done.1), kind=kOutput, calls=%fused_computation.94 | convolution fusion | flops 103809024 | bytes 4800512 | tf_op jit(solution)/shard_map/oc,pcxy->poxy/dot_general | solution.py:29
  107.2 2.2 %fusion.73 = f32[2,24,256,64]{2,3,1,0:T(8,128)} fusion(bf16[2,64,1,256]{3,1,2,0:T(8,128)(2,1)S(1)} %collective-permute-done.3, bf16[2,64,24,256]{3,1,2,0:T(8,128)(2,1)S(1)} %fusion.15, bf16[3,3,64,64]{3,2,1,0:T(8,128)(2,1)S(1)} %copy-done.1), kind=kOutput, calls=%fused_computation.83 | convolution fusion | flops 103809024 | bytes 4800512 | tf_op jit(solution)/shard_map/oc,pcxy->poxy/dot_general | solution.py:29
  109.4 5.9 %fusion.16 = bf16[2,64,24,256]{3,1,2,0:T(8,128)(2,1)S(1)} fusion(f32[2,24,256,64]{2,3,1,0:T(8,128)} %fusion.73, f32[2,24,256,64]{2,3,1,0:T(8,128)S(1)} %fusion.75, f32[2,24,256,64]{2,3,1,0:T(8,128)S(1)} %fusion.77, f32[2,24,256,64]{2,3,1,0:T(8,128)S(1)} %fusion.101, f32[2,24,256,64]{2,3,1,0:T(8,128)S(1)} %fusion.79, f32[2,24,256,64]{2,3,1,0:T(8,128)} %fusion.81, ...), kind=kOutput, calls=%fused_computation.28 | convolution fusion | flops 110886912 | bytes 28327936 | tf_op jit(solution)/shard_map/oc,pcxy->poxy/dot_general | solution.py:29
  115.8 3.3 %collective-permute-start.5 = (bf16[2,64,1,256]{3,1,2,0:T(8,128)(2,1)S(1)}, bf16[2,64,1,256]{3,1,2,0:T(8,128)(2,1)S(1)}, u32[]{:S(2)}, u32[]{:S(2)}) collective-permute-start(bf16[2,64,1,256]{3,1,2,0:T(8,128)(2,1)S(1)} %get-tuple-element.17), channel_id=1, source_target_pairs={{4,0},{8,4},{12,8},{0,12},{5,1},{9,5},{13,9},{1,13},{6,2},{10,6},{... | collective-permute-start | bytes 196616 | tf_op jit(solution)/shard_map/ppermute | solution.py:16
  119.9 1.6 collective-permute-done.4
  121.4 1.8 %select_maximum_fusion = bf16[2,64,26,258]{3,1,2,0:T(8,128)(2,1)S(1)} fusion(bf16[2,64,1,256]{3,1,2,0:T(8,128)(2,1)S(1)} %collective-permute-done.5, bf16[2,64,24,256]{3,1,2,0:T(8,128)(2,1)S(1)} %fusion.16, bf16[2,64,1,256]{3,1,2,0:T(8,128)(2,1)S(1)} %collective-permute-done.4), kind=kLoop, calls=%fused_computation.31 | loop fusion | flops 10303488 | bytes 3421184 | tf_op jit(solution)/shard_map/concatenate | solution.py:17
  123.2 2.5 %fusion.59 = f32[2,24,256,69]{2,3,1,0:T(8,128)} fusion(bf16[2,64,26,258]{3,1,2,0:T(8,128)(2,1)S(1)} %select_maximum_fusion, bf16[3,3,69,64]{2,3,1,0:T(8,128)(2,1)S(1)} %copy-done.2), kind=kOutput, calls=%fused_computation.70 | convolution fusion | flops 108527616 | bytes 4980736 | tf_op jit(solution)/shard_map/oc,pcxy->poxy/dot_general | solution.py:29
  125.7 2.6 %fusion.61 = f32[2,24,256,69]{2,3,1,0:T(8,128)} fusion(bf16[2,64,26,258]{3,1,2,0:T(8,128)(2,1)S(1)} %select_maximum_fusion, bf16[3,3,69,64]{2,3,1,0:T(8,128)(2,1)S(1)} %copy-done.2), kind=kOutput, calls=%fused_computation.72 | convolution fusion | flops 108527616 | bytes 4980736 | tf_op jit(solution)/shard_map/oc,pcxy->poxy/dot_general | solution.py:29
  128.3 2.5 %fusion.63 = f32[2,24,256,69]{2,3,1,0:T(8,128)} fusion(bf16[2,64,26,258]{3,1,2,0:T(8,128)(2,1)S(1)} %select_maximum_fusion, bf16[3,3,69,64]{2,3,1,0:T(8,128)(2,1)S(1)} %copy-done.2), kind=kOutput, calls=%fused_computation.74 | convolution fusion | flops 108527616 | bytes 4980736 | tf_op jit(solution)/shard_map/oc,pcxy->poxy/dot_general | solution.py:29
  130.8 2.5 %fusion.65 = f32[2,24,256,69]{2,3,1,0:T(8,128)} fusion(bf16[2,64,26,258]{3,1,2,0:T(8,128)(2,1)S(1)} %select_maximum_fusion, bf16[3,3,69,64]{2,3,1,0:T(8,128)(2,1)S(1)} %copy-done.2), kind=kOutput, calls=%fused_computation.76 | convolution fusion | flops 108527616 | bytes 4980736 | tf_op jit(solution)/shard_map/oc,pcxy->poxy/dot_general | solution.py:29
  133.3 2.4 %fusion.67 = f32[2,24,256,69]{2,3,1,0:T(8,128)} fusion(bf16[2,64,26,258]{3,1,2,0:T(8,128)(2,1)S(1)} %select_maximum_fusion, bf16[3,3,69,64]{2,3,1,0:T(8,128)(2,1)S(1)} %copy-done.2), kind=kOutput, calls=%fused_computation.78 | convolution fusion | flops 108527616 | bytes 4980736 | tf_op jit(solution)/shard_map/oc,pcxy->poxy/dot_general | solution.py:29
  135.7 2.4 %fusion.47 = f32[2,24,256,69]{2,3,1,0:T(8,128)} fusion(bf16[2,64,24,256]{3,1,2,0:T(8,128)(2,1)S(1)} %fusion.16, bf16[2,64,1,256]{3,1,2,0:T(8,128)(2,1)S(1)} %collective-permute-done.4, bf16[3,3,69,64]{2,3,1,0:T(8,128)(2,1)S(1)} %copy-done.2), kind=kOutput, calls=%fused_computation.60 | convolution fusion | flops 111804416 | bytes 5046272 | tf_op jit(solution)/shard_map/oc,pcxy->poxy/dot_general | solution.py:29
  138.1 2.4 %fusion.51 = f32[2,24,256,69]{2,3,1,0:T(8,128)} fusion(bf16[2,64,1,256]{3,1,2,0:T(8,128)(2,1)S(1)} %collective-permute-done.5, bf16[2,64,24,256]{3,1,2,0:T(8,128)(2,1)S(1)} %fusion.16, bf16[3,3,69,64]{2,3,1,0:T(8,128)(2,1)S(1)} %copy-done.2), kind=kOutput, calls=%fused_computation.64 | convolution fusion | flops 111804416 | bytes 5046272 | tf_op jit(solution)/shard_map/oc,pcxy->poxy/dot_general | solution.py:29
  140.5 10.2 %fusion.3 = bf16[2,69,24,256]{3,1,2,0:T(8,128)(2,1)S(1)} fusion(f32[2,24,256,69]{2,3,1,0:T(8,128)} %fusion.51, f32[2,24,256,69]{2,3,1,0:T(8,128)} %fusion.59, f32[2,24,256,69]{2,3,1,0:T(8,128)} %fusion.61, f32[2,24,256,69]{2,3,1,0:T(8,128)S(1)} %fusion.91, f32[2,24,256,69]{2,3,1,0:T(8,128)} %fusion.63, f32[2,24,256,69]{2,3,1,0:T(8,128)} %fusion.65, ...), kind=kOutput, calls=%fused_computation.11 | convolution fusion | flops 122941440 | bytes 34055168 | tf_op jit(solution)/shard_map/oc,pcxy->poxy/dot_general | solution.py:29
  150.7 1.5 copy.21
  (57 shorter events, 16.6 us)
Async XLA Ops:
  7.2 2.2 %copy-start.8 = (u32[32]{0:T(128)S(1)}, u32[32]{0:T(128)}, u32[]{:S(2)}) copy-start(u32[32]{0:T(128)} %constant.60) | copy-start | bytes 388
  7.2 3.4 %copy-start = (bf16[2,69,24,256]{3,2,1,0:T(8,128)(2,1)S(1)}, bf16[2,69,24,256]{3,2,1,0:T(8,128)(2,1)}, u32[]{:S(2)}) copy-start(bf16[2,69,24,256]{3,2,1,0:T(8,128)(2,1)} %param.9) | copy-start | bytes 5087236
  7.2 3.4 %copy-start.5 = (s32[24,256]{1,0:T(8,128)S(1)}, s32[24,256]{1,0:T(8,128)}, u32[]{:S(2)}) copy-start(s32[24,256]{1,0:T(8,128)} %param.12) | copy-start | bytes 73732
  7.2 3.4 %copy-start.4 = (f32[24,256]{1,0:T(8,128)S(1)}, f32[24,256]{1,0:T(8,128)}, u32[]{:S(2)}) copy-start(f32[24,256]{1,0:T(8,128)} %param.11) | copy-start | bytes 73732
  7.2 54.4 %all-gather.3.cloned.1.call-start = ((), (), s32[]{:S(2)}) async-start(), calls=%async_computation | async-start | bytes 8478720 | tf_op jit(solution)/shard_map/all_gather | solution.py:55
  7.9 17.2 %copy-start.7 = (u32[32]{0:T(128)S(1)}, u32[32]{0:T(128)}, u32[]{:S(2)}) copy-start(u32[32]{0:T(128)} %constant.65) | copy-start | bytes 388
  8.0 29.9 %copy-start.6 = (s32[2]{0:T(128)S(1)}, s32[2]{0:T(128)}, u32[]{:S(2)}) copy-start(s32[2]{0:T(128)} %param.13) | copy-start | bytes 28
  65.2 4.4 %copy-start.3 = (bf16[3,3,64,69]{3,2,1,0:T(8,128)(2,1)S(1)}, bf16[3,3,64,69]{3,2,1,0:T(8,128)(2,1)}, u32[]{:S(2)}) copy-start(bf16[3,3,64,69]{3,2,1,0:T(8,128)(2,1)} %param.15) | copy-start | bytes 238468
  65.7 6.7 %collective-permute-start = (bf16[2,69,1,256]{3,1,2,0:T(8,128)(2,1)S(1)}, bf16[2,69,1,256]{3,1,2,0:T(8,128)(2,1)S(1)}, u32[]{:S(2)}, u32[]{:S(2)}) collective-permute-start(bf16[2,69,1,256]{3,1,2,0:T(8,128)(2,1)S(1)} %get-tuple-element.14), channel_id=1, source_target_pairs={{0,4},{4,8},{8,12},{12,0},{1,5},{5,9},{9,13},{13,1},{2,6},{6,10},{... | collective-permute-start | bytes 211976 | tf_op jit(solution)/shard_map/ppermute | solution.py:13
  67.2 5.7 %collective-permute-start.1 = (bf16[2,69,1,256]{3,1,2,0:T(8,128)(2,1)S(1)}, bf16[2,69,1,256]{3,1,2,0:T(8,128)(2,1)S(1)}, u32[]{:S(2)}, u32[]{:S(2)}) collective-permute-start(bf16[2,69,1,256]{3,1,2,0:T(8,128)(2,1)S(1)} %get-tuple-element.15), channel_id=1, source_target_pairs={{4,0},{8,4},{12,8},{0,12},{5,1},{9,5},{13,9},{1,13},{6,2},{10,6},{... | collective-permute-start | bytes 211976 | tf_op jit(solution)/shard_map/ppermute | solution.py:16
  84.4 9.9 %copy-start.1 = (bf16[3,3,64,64]{3,2,1,0:T(8,128)(2,1)S(1)}, bf16[3,3,64,64]{3,2,1,0:T(8,128)(2,1)}, u32[]{:S(2)}) copy-start(bf16[3,3,64,64]{3,2,1,0:T(8,128)(2,1)} %param.16) | copy-start | bytes 221188
  90.5 6.3 %collective-permute-start.2 = (bf16[2,64,1,256]{3,1,2,0:T(8,128)(2,1)S(1)}, bf16[2,64,1,256]{3,1,2,0:T(8,128)(2,1)S(1)}, u32[]{:S(2)}, u32[]{:S(2)}) collective-permute-start(bf16[2,64,1,256]{3,1,2,0:T(8,128)(2,1)S(1)} %get-tuple-element.18), channel_id=1, source_target_pairs={{0,4},{4,8},{8,12},{12,0},{1,5},{5,9},{9,13},{13,1},{2,6},{6,10},{... | collective-permute-start | bytes 196616 | tf_op jit(solution)/shard_map/ppermute | solution.py:13
  91.6 5.2 %collective-permute-start.3 = (bf16[2,64,1,256]{3,1,2,0:T(8,128)(2,1)S(1)}, bf16[2,64,1,256]{3,1,2,0:T(8,128)(2,1)S(1)}, u32[]{:S(2)}, u32[]{:S(2)}) collective-permute-start(bf16[2,64,1,256]{3,1,2,0:T(8,128)(2,1)S(1)} %get-tuple-element.19), channel_id=1, source_target_pairs={{4,0},{8,4},{12,8},{0,12},{5,1},{9,5},{13,9},{1,13},{6,2},{10,6},{... | collective-permute-start | bytes 196616 | tf_op jit(solution)/shard_map/ppermute | solution.py:16
  109.4 9.8 %copy-start.2 = (bf16[3,3,69,64]{2,3,1,0:T(8,128)(2,1)S(1)}, bf16[3,3,69,64]{2,3,1,0:T(8,128)(2,1)}, u32[]{:S(2)}) copy-start(bf16[3,3,69,64]{2,3,1,0:T(8,128)(2,1)} %param.17) | copy-start | bytes 238468
  115.3 6.2 %collective-permute-start.4 = (bf16[2,64,1,256]{3,1,2,0:T(8,128)(2,1)S(1)}, bf16[2,64,1,256]{3,1,2,0:T(8,128)(2,1)S(1)}, u32[]{:S(2)}, u32[]{:S(2)}) collective-permute-start(bf16[2,64,1,256]{3,1,2,0:T(8,128)(2,1)S(1)} %get-tuple-element.16), channel_id=1, source_target_pairs={{0,4},{4,8},{8,12},{12,0},{1,5},{5,9},{9,13},{13,1},{2,6},{6,10},{... | collective-permute-start | bytes 196616 | tf_op jit(solution)/shard_map/ppermute | solution.py:13
  115.8 5.6 %collective-permute-start.5 = (bf16[2,64,1,256]{3,1,2,0:T(8,128)(2,1)S(1)}, bf16[2,64,1,256]{3,1,2,0:T(8,128)(2,1)S(1)}, u32[]{:S(2)}, u32[]{:S(2)}) collective-permute-start(bf16[2,64,1,256]{3,1,2,0:T(8,128)(2,1)S(1)} %get-tuple-element.17), channel_id=1, source_target_pairs={{4,0},{8,4},{12,8},{0,12},{5,1},{9,5},{13,9},{1,13},{6,2},{10,6},{... | collective-permute-start | bytes 196616 | tf_op jit(solution)/shard_map/ppermute | solution.py:16
Sparse Core Ops, SparseCore 0:
  9.6 51.9 all-gather.2
